TPU v7x, 32 devices: a whole 2x2x4 slice. The times are simulated.
32 devices in a mesh: grp: 2 (over y), tile: 4 (over z), row: 2 (over x), sub: 2 (over core).
Axes of the slice: x: 2, y: 2, z: 4, core: 2. Of those that a mesh axis runs over, the one named last changes fastest.
Arguments:
- velocity: float32 [2, 480, 960], P(None, ('grp', 'row'), ('tile', 'sub')), parts along dimension 1, may hold values from -10 to 10, as said below
- wet_bits: int32 [16, 960], P(('grp', 'row'), ('tile', 'sub')), parts along dimension 0, may hold values from 0 to 1073741823, as said below
- east_face: int32 [4], replicated, may hold values from 0 to 3, as said below
- seam_turn: int32 [4], replicated, may hold values from 0 to 3
Outputs:
- forcing: float32 [2, 120, 240], P(None, ('grp', 'row'), ('tile', 'sub')), parts along dimension 1
There are 2 independent parts, one for each index of `grp`. A program takes and returns all parts, laid end to end along the dimension named above; an argument that names none is the same for every part. Nothing has to cross between parts.
Inputs may be any that keep to these rules, and one draw needn't show every extreme that they name: `velocity`: gentle combinations of a few waves plus independent cell-to-cell parts. Bit b of wet_bits[j, x] is 1 where cell (30 j + b, x) is wet and 0 on land. `east_face`: each face is east of exactly one face.
All inputs are finite; a program needn't handle non-finite values.
Results may differ from a plain program's by a relative error of at most 0.000098.
Values sent between devices are 32-bit elements; how exact they have to be, the bound alone decides.
No kernel may reach another device: no remote copies, remote signals or barrier semaphores. Data moves between devices by JAX's collectives and lax.ppermute only.
A program may use at most 64 MiB of HBM per device.

v0:
```python
import jax
import jax.numpy as jnp
from jax import lax
from jax.sharding import PartitionSpec as P

R = 32


deriv_scale = 8.0


def with_halo(value, sides, width, wrap):
    for axis, dim in sides:
        count, length = (lax.axis_size(axis), value.shape[dim])
        up = [(i, (i + 1) % count) for i in range(count if wrap else count - 1)]
        down = [(j, i) for i, j in up]
        last = lax.slice_in_dim(value, length - width, length, axis=dim)
        first = lax.slice_in_dim(value, 0, width, axis=dim)
        before = lax.ppermute(last, axis, up)
        after = lax.ppermute(first, axis, down)
        value = jnp.concatenate([before, value, after], axis=dim)
    return value


def unpack(wet_bits):
    repeated = jnp.repeat(wet_bits, 30, axis=0)
    shifts = lax.broadcasted_iota(jnp.int32, repeated.shape, 0) % 30
    return (jnp.right_shift(repeated, shifts) & 1).astype(jnp.float32)


def banded(n_in, n_out):
    offset = (
        jnp.arange(n_in, dtype=jnp.int32)[:, None] - jnp.arange(n_out, dtype=jnp.int32)[None, :]
    )
    spread = R * 1.0
    centred = (offset - R).astype(jnp.float32)
    taps = (jnp.arange(2 * R + 1, dtype=jnp.int32) - R).astype(jnp.float32)
    weight_sum = jnp.sum(jnp.exp(-0.5 * (taps / spread) ** 2))
    inside = (offset >= 0) & (offset <= 2 * R)
    return jnp.where(inside, jnp.exp(-0.5 * (centred / spread) ** 2) / weight_sum, jnp.float32(0.0))


def rotate(strip, turn):
    cosine = jnp.where(turn == 0, 1.0, jnp.where(turn == 2, -1.0, 0.0)).astype(jnp.float32)
    sine_part = jnp.where(turn == 1, 1.0, jnp.where(turn == 3, -1.0, 0.0)).astype(jnp.float32)
    return jnp.stack(
        [cosine * strip[0] - sine_part * strip[1], sine_part * strip[0] + cosine * strip[1]]
    )


def derive(padded):
    centre = padded[:, 1:-1, ..., 1:-1]
    grad_x = deriv_scale * (padded[:, 1:-1, ..., 2:] - padded[:, 1:-1, ..., :-2])
    grad_y = deriv_scale * (padded[:, 2:, ..., 1:-1] - padded[:, :-2, ..., 1:-1])
    advect = centre[0] * grad_x + centre[1] * grad_y
    return jnp.concatenate([centre, grad_x, grad_y, advect], axis=0)


def combine(smooth):
    east_part = smooth[6] - (smooth[0] * smooth[2] + smooth[1] * smooth[4])
    north_part = smooth[7] - (smooth[0] * smooth[3] + smooth[1] * smooth[5])
    return jnp.stack([east_part, north_part])


def pick(table, index):
    return lax.dynamic_index_in_dim(table, index, 0, keepdims=False)


def on_device(velocity, wet_bits, east_face, seam_turn):
    n_rows = velocity.shape[1]
    n_cols = velocity.shape[2]
    wet = unpack(wet_bits)
    field = velocity * wet[None]
    rim_width = R + 1
    row_count = lax.axis_size("row")
    tile_at = lax.axis_index("tile")
    sub_at = lax.axis_index("sub")
    row_at = lax.axis_index("row")
    face_count = east_face.shape[0]
    y_depth = R + 1
    extended = with_halo(field, (("row", 1),), R + 1, False)
    face_ids = jnp.arange(face_count, dtype=jnp.int32)
    west_face = jnp.sum(jnp.where(east_face == tile_at, face_ids, 0))
    east_next = pick(east_face, tile_at)
    east_turn = pick(seam_turn, tile_at)
    west_turn = (4 - pick(seam_turn, west_face)) % 4
    inner = with_halo(extended, (("sub", 2),), rim_width, True)
    west_rim = inner[:, :, :rim_width]
    east_rim = inner[:, :, n_cols + rim_width :]
    outer = jnp.where(sub_at == 0, west_rim, east_rim)
    gathered = lax.all_gather(outer[None], "tile", axis=0, tiled=True)
    seam_west = rotate(pick(gathered, west_face), west_turn)
    seam_east = rotate(pick(gathered, east_next), east_turn)
    from_west = jnp.where(sub_at == 0, seam_west, west_rim)
    from_east = jnp.where(sub_at == 1, seam_east, east_rim)
    padded = jnp.concatenate([from_west, extended, from_east], axis=2)
    channels = derive(padded)
    global_row = row_at * n_rows - R + jnp.arange(n_rows + 2 * R, dtype=jnp.int32)
    valid = ((global_row >= 0) & (global_row < row_count * n_rows)).astype(jnp.float32)
    channels = channels * valid[None, :, None]
    along = jnp.einsum(
        "cyx,xj->cyj", channels, banded(n_cols + 2 * R, n_cols), precision=lax.Precision.HIGHEST
    )
    smooth = jnp.einsum(
        "ki,ckx->cix", banded(n_rows + 2 * R, n_rows), along, precision=lax.Precision.HIGHEST
    )
    fine = combine(smooth) * wet[None]
    return fine.reshape(2, n_rows // 4, 4, n_cols // 4, 4).mean(axis=(2, 4))


def solution(mesh):
    placed = (
        P(None, ("grp", "row"), ("tile", "sub")),
        P(("grp", "row"), ("tile", "sub")),
        P(),
        P(),
    )
    return jax.shard_map(
        on_device,
        mesh=mesh,
        in_specs=placed,
        out_specs=P(None, ("grp", "row"), ("tile", "sub")),
        check_vma=False,
    )
```

profile of v0, /device:TPU:0, one launch (start us, length us, event | category | flops | bytes accessed | tf_op | source)
XLA Modules:
  0.0 54.4 jit_solution(6808391245389461637)
XLA Ops:
  0.0 0.7 %broadcast_in_dim.23 = s32[4,30,120]{2,1,0:T(8,128)S(1)} broadcast(s32[4,120]{1,0:T(4,128)} %param.5), dimensions={0,2} | broadcast | bytes 59520 | tf_op jit(solution)/shard_map/broadcast_in_dim | solution.py:26
  0.9 1.0 %copy.22 = f32[2,120,120]{1,2,0:T(8,128)S(1)} copy(f32[2,120,120]{2,1,0:T(8,128)} %param.4) | data formatting | bytes 230400 | tf_op args[0]
  2.1 4.9 %collective-permute-start = (f32[2,33,120]{1,2,0:T(8,128)S(1)}, f32[2,33,120]{1,2,0:T(8,128)S(1)}, u32[]{:S(2)}, u32[]{:S(2)}) collective-permute-start(f32[2,33,120]{1,2,0:T(8,128)S(1)} %get-tuple-element.19), channel_id=1, source_target_pairs={{0,2},{1,3},{4,6},{5,7},{8,10},{9,11},{12,14},{13,15},{16,18},{17,... | collective-permute-start | bytes 95048 | tf_op jit(solution)/shard_map/ppermute | solution.py:19
  6.9 1.3 %collective-permute-start.1 = (f32[2,33,120]{1,2,0:T(8,128)S(1)}, f32[2,33,120]{1,2,0:T(8,128)S(1)}, u32[]{:S(2)}, u32[]{:S(2)}) collective-permute-start(f32[2,33,120]{1,2,0:T(8,128)S(1)} %get-tuple-element.20), channel_id=1, source_target_pairs={{2,0},{3,1},{6,4},{7,5},{10,8},{11,9},{14,12},{15,13},{18,16},{19,... | collective-permute-start | bytes 95048 | tf_op jit(solution)/shard_map/ppermute | solution.py:20
  8.3 3.2 %reshape.215 = s32[30,4,30,4]{3,2,1,0:T(8,128)} reshape(s32[4,30,120]{2,1,0:T(8,128)S(1)} %broadcast_in_dim.23) | data formatting | bytes 115200 | tf_op jit(solution)/shard_map/reshape | solution.py:26
  11.5 1.8 %and_convert_fusion = f32[30,4,30,4]{3,2,1,0:T(8,128)S(1)} fusion(s32[30,4,30,4]{3,2,1,0:T(8,128)} %reshape.215, s32[30,4]{1,0:T(8,128)S(1)} %get-tuple-element.25, s32[30,4]{1,0:T(8,128)S(1)} %get-tuple-element.26, pred[30,4]{1,0:T(8,128)(4,1)S(1)} %compare_and_fusion), kind=kLoop, calls=%fused_computation | loop fusion | flops 57600 | bytes 116280 | tf_op jit(solution)/shard_map/convert_element_type | solution.py:28
  13.4 0.6 %fusion.23 = s32[]{:T(128)} fusion(s32[4]{0:T(128)S(1)} %copy-done.1, s32[]{:T(128)S(6)} %axis_index.35), kind=kLoop, calls=%fused_computation.59 | loop fusion | flops 11 | bytes 24 | tf_op jit(solution)/shard_map/reduce_sum | solution.py:83
  14.2 0.5 collective-permute-start.3
  14.7 0.7 %dynamic_slice.20 = s32[1]{0:T(128)} dynamic-slice(s32[4]{0:T(128)S(1)} %copy-done.1, s32[]{:T(128)S(6)} %select_n.106), dynamic_slice_sizes={1} | dynamic-slice | bytes 12 | tf_op jit(solution)/shard_map/jit(dynamic_index_in_dim)/dynamic_slice | solution.py:66
  18.7 0.6 %fusion.37 = (s32[1]{0:T(128)}, s32[1]{0:T(128)}) fusion(s32[4]{0:T(128)S(1)} %copy-done, s32[]{:T(128)S(6)} %select_n.96, s32[]{:T(128)S(6)} %select_n.106), kind=kLoop, calls=%fused_computation.76 | loop fusion | bytes 24 | tf_op jit(solution)/shard_map/jit(dynamic_index_in_dim)/dynamic_slice | solution.py:66
  22.3 0.8 %copy.28 = f32[30,4,30,4]{2,3,1,0:T(4,128)S(1)} copy(f32[30,4,30,4]{3,2,1,0:T(8,128)S(1)} %and_convert_fusion) | data formatting | bytes 115200 | tf_op jit(solution)/shard_map/convert_element_type | solution.py:28
  23.8 0.6 %exponential_reduce_fusion = f32[]{:T(128)} fusion(), kind=kLoop, calls=%fused_computation.60 | loop fusion | flops 389 | bytes 4 | tf_op jit(solution)/shard_map/reduce_sum | solution.py:38
  24.4 14.5 %all-gather = f32[8,186,33]{1,2,0:T(8,128)S(1)} all-gather(f32[2,186,33]{1,2,0:T(8,128)S(1)} %broadcast_select_fusion), channel_id=2, replica_groups=mesh['grp'=2,'tile'=4,'row'=2,'sub'=2] {'tile'}, dimensions={0}, use_global_device_ids=true | all-gather | bytes 245520 | tf_op jit(solution)/shard_map/all_gather | solution.py:91
  39.0 0.2 pad_maximum_fusion
  39.2 0.2 fusion.10
  39.4 0.5 fusion.35
  39.8 3.5 %fusion = f32[8,184,120]{2,1,0:T(8,128)S(1)} fusion(f32[2,184,184]{1,2,0:T(8,128)S(1)} %get-tuple-element.8, f32[2,184,184]{1,2,0:T(8,128)S(1)} %get-tuple-element.9, f32[2,184,184]{1,2,0:T(8,128)S(1)} %get-tuple-element.10, f32[2,184,184]{1,2,0:T(8,128)S(1)} %get-tuple-element.7, f32[184]{0:T(256)S(1)} %and_convert_fusion.2, f32[]{:T(128)} %exponential_reduce_fusion), kind=kOutput, calls=%fused_computation.2 | convolution fusion | flops 391347392 | bytes 1790692 | tf_op jit(solution)/shard_map/cyx,xj->cyj/dot_general | solution.py:101
  43.4 2.3 %convolution_bitcast_fusion = f32[8,120,120]{1,2,0:T(8,128)S(1)} fusion(f32[8,184,120]{2,1,0:T(8,128)S(1)} %fusion, f32[]{:T(128)} %exponential_reduce_fusion), kind=kOutput, calls=%fused_computation.9 | convolution fusion | flops 254604480 | bytes 1167364 | tf_op jit(solution)/shard_map/ki,ckx->cix/dot_general | solution.py:104
  45.8 1.9 %reshape.218 = f32[1,30,4,30,4]{2,1,4,3,0:T(8,128)S(1)} reshape(f32[1,120,120]{1,2,0:T(8,128)S(1)} %get-tuple-element.5) | data formatting | bytes 115200 | tf_op jit(solution)/shard_map/stack | solution.py:62
  47.7 1.9 %copy.26 = f32[1,30,4,30,4]{3,4,2,1,0:T(4,128)S(1)} copy(f32[1,30,4,30,4]{2,1,4,3,0:T(8,128)S(1)} %reshape.218) | data formatting | bytes 115200 | tf_op jit(solution)/shard_map/stack | solution.py:62
  49.6 1.9 %reshape.219 = f32[1,30,4,30,4]{2,1,4,3,0:T(8,128)S(1)} reshape(f32[1,120,120]{1,2,0:T(8,128)S(1)} %get-tuple-element.6) | data formatting | bytes 115200 | tf_op jit(solution)/shard_map/stack | solution.py:62
  51.5 1.9 %copy.27 = f32[1,30,4,30,4]{3,4,2,1,0:T(4,128)S(1)} copy(f32[1,30,4,30,4]{2,1,4,3,0:T(8,128)S(1)} %reshape.219) | data formatting | bytes 115200 | tf_op jit(solution)/shard_map/stack | solution.py:62
  53.4 0.3 fusion.8
  53.7 0.6 %copy.30 = f32[2,30,30]{2,0,1:T(2,128)} copy(f32[2,30,30]{2,1,0:T(8,128)S(1)} %broadcast_multiply_fusion.3) | data formatting | bytes 14400 | tf_op jit(solution)/shard_map/div | solution.py:108
  (26 shorter events, 0.7 us)
Async XLA Ops:
  2.1 12.0 %collective-permute-start = (f32[2,33,120]{1,2,0:T(8,128)S(1)}, f32[2,33,120]{1,2,0:T(8,128)S(1)}, u32[]{:S(2)}, u32[]{:S(2)}) collective-permute-start(f32[2,33,120]{1,2,0:T(8,128)S(1)} %get-tuple-element.19), channel_id=1, source_target_pairs={{0,2},{1,3},{4,6},{5,7},{8,10},{9,11},{12,14},{13,15},{16,18},{17,... | collective-permute-start | bytes 95048 | tf_op jit(solution)/shard_map/ppermute | solution.py:19
  6.9 7.1 %collective-permute-start.1 = (f32[2,33,120]{1,2,0:T(8,128)S(1)}, f32[2,33,120]{1,2,0:T(8,128)S(1)}, u32[]{:S(2)}, u32[]{:S(2)}) collective-permute-start(f32[2,33,120]{1,2,0:T(8,128)S(1)} %get-tuple-element.20), channel_id=1, source_target_pairs={{2,0},{3,1},{6,4},{7,5},{10,8},{11,9},{14,12},{15,13},{18,16},{19,... | collective-permute-start | bytes 95048 | tf_op jit(solution)/shard_map/ppermute | solution.py:20
  11.5 1.9 %copy-start.1 = (s32[4]{0:T(128)S(1)}, s32[4]{0:T(128)}, u32[]{:S(2)}) copy-start(s32[4]{0:T(128)} %param.6) | copy-start | bytes 52
  11.5 7.2 %copy-start = (s32[4]{0:T(128)S(1)}, s32[4]{0:T(128)}, u32[]{:S(2)}) copy-start(s32[4]{0:T(128)} %param.7) | copy-start | bytes 52
  14.2 10.3 %collective-permute-start.2 = (f32[2,186,33]{1,2,0:T(8,128)S(1)}, f32[2,186,33]{1,2,0:T(8,128)S(1)}, u32[]{:S(2)}, u32[]{:S(2)}) collective-permute-start(f32[2,186,33]{1,2,0:T(8,128)S(1)} %get-tuple-element.13), channel_id=1, source_target_pairs={{0,1},{1,0},{2,3},{3,2},{4,5},{5,4},{6,7},{7,6},{8,9},{9,8},{10,11... | collective-permute-start | bytes 147320 | tf_op jit(solution)/shard_map/ppermute | solution.py:19
  14.2 10.2 %collective-permute-start.3 = (f32[2,186,33]{1,2,0:T(8,128)S(1)}, f32[2,186,33]{1,2,0:T(8,128)S(1)}, u32[]{:S(2)}, u32[]{:S(2)}) collective-permute-start(f32[2,186,33]{1,2,0:T(8,128)S(1)} %get-tuple-element.14), channel_id=1, source_target_pairs={{1,0},{0,1},{3,2},{2,3},{5,4},{4,5},{7,6},{6,7},{9,8},{8,9},{11,10... | collective-permute-start | bytes 147320 | tf_op jit(solution)/shard_map/ppermute | solution.py:20
where the time goes:
time: 55 us; the launch traced here: 54.4 us
  local copies, waits for them, and re-layouts  15.5 us (28%)
  blocking collectives  14.5 us (26%)
  between operations  7.18 us (13%)
  starting transfers between devices  6.74 us (12%)
  matrix products  5.89 us (11%)
  other arithmetic  4.56 us (8%)
    all_gather x1, blocking collectives, on_device(): gathered = lax.all_gather(outer[None], 'tile', axis=0, tiled=True)  14.5 us
    another operation x4, local copies, waits for them, and re-layouts, combine(): return jnp.stack([east_part, north_part])  7.64 us
    ppermute x2, starting transfers between devices, with_halo(): before = lax.ppermute(last, axis, up)  4.96 us
    dot_general x1, matrix products, on_device(): jnp.einsum('cyx,xj->cyj', channels, banded(n_cols + 2 * R, n_cols), preci...  3.54 us
    reshape x2, local copies, waits for them, and re-layouts, unpack(): repeated = jnp.repeat(wet_bits, 30, axis=0)  3.24 us
    dot_general x1, matrix products, on_device(): jnp.einsum('ki,ckx->cix', banded(n_rows + 2 * R, n_rows), along, precisio...  2.35 us
    convert_element_type x2, other arithmetic, unpack(): return (jnp.right_shift(repeated, shifts) & 1).astype(jnp.float32)  1.95 us
    ppermute x2, starting transfers between devices, with_halo(): after = lax.ppermute(first, axis, down)  1.79 us
  transfers between devices with their start and end apart: 4, of which 0 were waited for; matrix products, arithmetic and copies ran while one was open for 16% of the time, Pallas kernels for 0%

commit v1 on v0

v1 whole, which is shorter than its diff:
```python
import functools
import itertools

import jax
import jax.numpy as jnp
import numpy as np
from jax import lax
from jax.experimental import pallas as pl
from jax.experimental.pallas import tpu as pltpu
from jax.sharding import PartitionSpec as P

R = 32
RIM = R + 1
BITS = 30
COARSE = 4
LANES = 128
HALF = LANES // 2
SUBLANES = 8
SWITCHED_FACES = 4

deriv_scale = 8.0

f32 = jnp.float32
bf16 = jnp.bfloat16


def up_to(value, step):
    return -(-value // step) * step


def iota(shape, dim):
    return lax.broadcasted_iota(jnp.int32, shape, dim)


def split(value):
    high = value.astype(bf16)
    return high, (value - high.astype(f32)).astype(bf16)


def dot(left, right):
    return jnp.dot(left, right, preferred_element_type=f32)


def taps_sum():
    taps = np.arange(-R, R + 1, dtype=np.float64)
    return float(np.sum(np.exp(-0.5 * (taps / R) ** 2)))


def gaussian(distance, inside):
    inside = inside & (distance >= -R) & (distance <= R)
    scaled = distance.astype(f32) * (1.0 / R)
    return jnp.where(inside, jnp.exp(-0.5 * scaled * scaled) * (1.0 / taps_sum()), 0.0)


def roll(value, shift):
    return pltpu.roll(value, shift % LANES, axis=1)


def place(value, columns):
    return jnp.pad(value, ((0, 0), (0, columns - value.shape[1])))


def mask_kernel(geom, velocity, wet_bits, east_face, seam_turn, field, rows, wet, turn):
    n_rows, n_cols, depth, row_count, _ = geom
    at = iota((n_rows, n_cols), 0)
    word = jnp.zeros((n_rows, n_cols), jnp.int32)
    for j in range(n_rows // BITS):
        line = jnp.broadcast_to(wet_bits[j : j + 1, :], (n_rows, n_cols))
        word = jnp.where((at >= j * BITS) & (at < (j + 1) * BITS), line, word)
    bits = jnp.right_shift(word, at % BITS) & 1
    mask = bits.astype(f32)
    wet[:, :n_cols] = mask
    wet[:, n_cols:] = jnp.zeros((n_rows, LANES - n_cols), f32)
    row_at = lax.axis_index("row")
    for c in range(2):
        value = place(velocity[c] * mask, LANES)
        field[c] = value
        if row_count == 2:
            rows[c] = jnp.where(row_at == 0, value[n_rows - depth :], value[:depth])
        elif row_count > 2:
            rows[c, :depth] = value[:depth]
            rows[c, depth:] = value[n_rows - depth :]
    tile_at = lax.axis_index("tile")
    faces = east_face.shape[0]
    back = jnp.int32(0)
    for w in range(faces):
        back = jnp.where(east_face[w] == tile_at, seam_turn[w], back)
    ahead = seam_turn[tile_at]
    quarter = jnp.where(lax.axis_index("sub") == 0, (4 - back) % 4, ahead)
    cosine = jnp.where(quarter == 0, 1.0, jnp.where(quarter == 2, -1.0, 0.0)).astype(f32)
    sine = jnp.where(quarter == 1, 1.0, jnp.where(quarter == 3, -1.0, 0.0)).astype(f32)
    row = iota((SUBLANES, LANES), 0)
    lane = iota((SUBLANES, LANES), 1)
    turn[...] = jnp.where(row == 0, cosine, jnp.where(lane < HALF, -sine, sine))


def extend_kernel(geom, field, before, after, extended, outer, inner):
    n_rows, n_cols, depth, row_count, window = geom
    row_at = lax.axis_index("row")
    lane = iota((window, LANES), 1)
    whole = []
    for c in range(2):
        mine = field[c]
        if row_count == 2:
            other = before[c]
            value = jnp.where(
                row_at == 0,
                jnp.concatenate([mine, other], axis=0),
                jnp.concatenate([other, mine], axis=0),
            )
        elif row_count > 2:
            value = jnp.concatenate([before[c], mine, after[c]], axis=0)
        else:
            value = mine
        extended[c] = value
        whole.append(value)
    west = jnp.where(lane < HALF, whole[0], roll(whole[1], HALF))
    east = jnp.where(
        lane < HALF, roll(whole[0], RIM - n_cols), roll(whole[1], HALF + RIM - n_cols)
    )
    first = lax.axis_index("sub") == 0
    outer[...] = jnp.where(first, west, east)
    inner[...] = jnp.where(first, east, west)


def filter_kernel(geom, extended, seam, beside, wet, turn, forcing, columns, padded, along):
    n_rows, n_cols, depth, row_count, window = geom
    first = lax.axis_index("sub") == 0
    row_at = lax.axis_index("row")
    wide = 2 * LANES
    lane = iota((wide, LANES), 0)
    target = iota((wide, LANES), 1)
    rim = lane - LANES
    column = jnp.where(
        lane < LANES, lane, jnp.where(rim < HALF, rim - RIM, rim - HALF + n_cols)
    )
    inside = (
        (lane < n_cols)
        | ((rim >= 1) & (rim < RIM))
        | ((rim >= HALF) & (rim < HALF + R))
    )
    x_high, x_low = split(gaussian(column - target, inside & (target < n_cols)))
    x_both = jnp.concatenate([x_high, x_low], axis=1)
    out_rows = up_to(n_rows, 2 * SUBLANES)
    source = iota((out_rows, window), 1)
    target = iota((out_rows, window), 0)
    if row_count == 2:
        start = jnp.where(row_at == 0, 0, depth)
    elif row_count > 2:
        start = jnp.int32(depth)
    else:
        start = jnp.int32(0)
    world = source - start + row_at * n_rows
    inside = (world >= 0) & (world < row_count * n_rows) & (target < n_rows)
    y_high, y_low = split(gaussian(source - start - target, inside))
    y_both = jnp.concatenate([y_high, y_low], axis=0)

    lane = iota((window, LANES), 1)
    low = lane < HALF
    cosine = turn[0:1, :]
    sine = turn[1:2, :]
    got = seam[...]
    turned = cosine * got + sine * roll(got, HALF)
    near = beside[...]
    west = jnp.where(first, turned, near)
    east = jnp.where(first, near, turned)
    west_far = roll(west, HALF)
    east_far = roll(east, HALF)
    blank = jnp.zeros((SUBLANES, wide), f32)
    for c in range(2):
        own = extended[c]
        if c == 0:
            rims = jnp.where(low, west, east_far)
        else:
            rims = jnp.where(low, west_far, east)
        rims = jnp.where(lane == RIM, roll(own, RIM), rims)
        rims = jnp.where(lane == HALF - 1, roll(own, HALF - n_cols), rims)
        own = jnp.where(
            lane < n_cols,
            own,
            jnp.where(lane == n_cols, roll(rims, n_cols - HALF), roll(rims, LANES - RIM)),
        )
        padded[c, :SUBLANES, :] = blank
        padded[c, SUBLANES + window :, :] = blank
        padded[c, SUBLANES : SUBLANES + window, :LANES] = own
        padded[c, SUBLANES : SUBLANES + window, LANES:] = rims

    def store(c, part, value):
        high, low_part = split(value)
        columns[0, c, :, part * LANES : (part + 1) * LANES] = high
        columns[1, c, :, part * LANES : (part + 1) * LANES] = low_part

    for part in range(2):
        at = slice(part * LANES, (part + 1) * LANES)
        vel = [padded[c, SUBLANES : SUBLANES + window, at] for c in range(2)]
        grad_x = [roll(vel[c], -1) - roll(vel[c], 1) for c in range(2)]
        grad_y = [
            padded[c, SUBLANES + 1 : SUBLANES + 1 + window, at]
            - padded[c, SUBLANES - 1 : SUBLANES - 1 + window, at]
            for c in range(2)
        ]
        for c in range(2):
            store(c, part, vel[c])
            store(2 + c, part, grad_x[c])
            store(4 + c, part, grad_y[c])
            store(6 + c, part, vel[0] * grad_x[c] + vel[1] * grad_y[c])
    smooth = []
    for c in range(8):
        main = dot(columns[0, c], x_both)
        value = main[:, :LANES] + (main[:, LANES:] + dot(columns[1, c], x_high))
        high, low_part = split(value)
        pair, side = divmod(c, 2)
        along[0, pair, :, side * LANES : (side + 1) * LANES] = high
        along[1, pair, :, side * LANES : (side + 1) * LANES] = low_part
    for pair in range(4):
        main = dot(y_both, along[0, pair])
        value = main[:out_rows] + (main[out_rows:] + dot(y_high, along[1, pair]))
        smooth += [value[:n_rows, :LANES], value[:n_rows, LANES:]]
    mask = wet[...]
    fine = [
        mask * (smooth[6 + c] - (smooth[0] * smooth[2 + c] + smooth[1] * smooth[4 + c]))
        for c in range(2)
    ]
    both = jnp.concatenate(fine, axis=1)
    both = jnp.pad(both, ((0, out_rows - n_rows), (0, 0)))
    coarse = n_rows // COARSE
    coarse_rows = up_to(coarse, 2 * SUBLANES)
    block = iota((coarse_rows, out_rows), 1) // COARSE == iota((coarse_rows, out_rows), 0)
    gather_y = jnp.where(block, 1.0, 0.0).astype(bf16)
    high, low_part = split(both)
    pooled = dot(gather_y, high) + dot(gather_y, low_part)
    block = iota((LANES, LANES), 0) // COARSE == iota((LANES, LANES), 1)
    gather_x = jnp.where(block, deriv_scale / (COARSE * COARSE), 0.0).astype(bf16)
    for c in range(2):
        high, low_part = split(pooled[:, c * LANES : (c + 1) * LANES])
        value = dot(high, gather_x) + dot(low_part, gather_x)
        forcing[c] = value[:coarse, : n_cols // COARSE]


VMEM_SPEC = pl.BlockSpec(memory_space=pltpu.VMEM)
SMEM_SPEC = pl.BlockSpec(memory_space=pltpu.SMEM)


def seam_order(east_face):
    count = east_face.shape[0]
    one = iota((count, count), 0)
    two = iota((count, count), 1)
    weight = jnp.zeros((count, count), jnp.int32)
    for i in range(count):
        weight = jnp.where(one == i, int(np.prod(np.arange(1, count - i))), weight)
    smaller = (east_face[None, :] < east_face[:, None]) & (two > one)
    return jnp.sum(jnp.where(smaller, weight, 0))


def exchange(east_face, outer, inner):
    faces = east_face.shape[0]
    subs = lax.axis_size("sub")
    beside = [(i, subs - 1 - i) for i in range(subs)]

    def swap(order, outer, inner):
        pairs = []
        for west, east in enumerate(order):
            pairs += [(west * subs + subs - 1, east * subs), (east * subs, west * subs + subs - 1)]
        return (
            lax.ppermute(outer, ("tile", "sub"), pairs),
            lax.ppermute(inner, "sub", beside),
        )

    if faces <= SWITCHED_FACES:
        orders = itertools.permutations(range(faces))
        branches = [functools.partial(swap, order) for order in orders]
        return lax.switch(seam_order(east_face), branches, outer, inner)
    tile_at = lax.axis_index("tile")
    sub_at = lax.axis_index("sub")
    west = jnp.sum(jnp.where(east_face == tile_at, jnp.arange(faces, dtype=jnp.int32), 0))
    east = lax.dynamic_index_in_dim(east_face, tile_at, 0, keepdims=False)
    gathered = lax.all_gather(lax.ppermute(outer, "sub", beside), "tile")
    partner = jnp.where(sub_at == 0, west, east)
    seam = lax.dynamic_index_in_dim(gathered, partner, 0, keepdims=False)
    return seam, lax.ppermute(inner, "sub", beside)


def on_device(velocity, wet_bits, east_face, seam_turn):
    _, n_rows, n_cols = velocity.shape
    row_count = lax.axis_size("row")
    depth = up_to(RIM, SUBLANES)
    sides = min(row_count - 1, 2)
    window = n_rows + sides * depth
    geom = (n_rows, n_cols, depth, row_count, window)
    sent = depth * max(sides, 1)
    params = pltpu.CompilerParams(vmem_limit_bytes=16 << 20)
    shape = jax.ShapeDtypeStruct
    field, rows, wet, turn = pl.pallas_call(
        functools.partial(mask_kernel, geom),
        out_shape=(
            shape((2, n_rows, LANES), f32),
            shape((2, sent, LANES), f32),
            shape((n_rows, LANES), f32),
            shape((SUBLANES, LANES), f32),
        ),
        in_specs=[VMEM_SPEC, VMEM_SPEC, SMEM_SPEC, SMEM_SPEC],
        out_specs=(VMEM_SPEC,) * 4,
        compiler_params=params,
        name="mask",
    )(velocity, wet_bits, east_face, seam_turn)
    if row_count == 2:
        before = lax.ppermute(rows, "row", [(0, 1), (1, 0)])
        after = before
    elif row_count > 2:
        up = [(i, i + 1) for i in range(row_count - 1)]
        before = lax.ppermute(rows[:, depth:], "row", up)
        after = lax.ppermute(rows[:, :depth], "row", [(j, i) for i, j in up])
    else:
        before = after = rows
    extended, outer, inner = pl.pallas_call(
        functools.partial(extend_kernel, geom),
        out_shape=(
            shape((2, window, LANES), f32),
            shape((window, LANES), f32),
            shape((window, LANES), f32),
        ),
        in_specs=[VMEM_SPEC] * 3,
        out_specs=(VMEM_SPEC,) * 3,
        compiler_params=params,
        name="extend",
    )(field, before, after)
    seam, beside = exchange(east_face, outer, inner)
    wide = 2 * LANES
    return pl.pallas_call(
        functools.partial(filter_kernel, geom),
        out_shape=shape((2, n_rows // COARSE, n_cols // COARSE), f32),
        in_specs=[VMEM_SPEC] * 5,
        out_specs=VMEM_SPEC,
        scratch_shapes=[
            pltpu.VMEM((2, 8, window, wide), bf16),
            pltpu.VMEM((2, window + 2 * SUBLANES, wide), f32),
            pltpu.VMEM((2, 4, window, wide), bf16),
        ],
        compiler_params=params,
        name="filter",
    )(extended, seam, beside, wet, turn)


def solution(mesh):
    placed = (
        P(None, ("grp", "row"), ("tile", "sub")),
        P(("grp", "row"), ("tile", "sub")),
        P(),
        P(),
    )
    return jax.shard_map(
        on_device,
        mesh=mesh,
        in_specs=placed,
        out_specs=P(None, ("grp", "row"), ("tile", "sub")),
        check_vma=False,
    )
```

time: 55 us -> 17.2 us (0.31)
  blocking collectives: 14.5 us -> 0 us
  local copies, waits for them, and re-layouts: 15.5 us -> 3.53 us
  between operations: 7.18 us -> 0.68 us
  matrix products: 5.89 us -> 0 us
  other arithmetic: 4.56 us -> 0.72 us
  Pallas kernels: 0 us -> 3.25 us
  waiting for transfers between devices: 0.01 us -> 2.34 us
    all_gather x1 -> x0, blocking collectives: 14.5 us -> none  [on_device(): gathered = lax.all_gather(outer[None], 'tile', axis=0, tiled=True)]
    another operation x4 -> x0, local copies, waits for them, and re-layouts: 7.64 us -> none  [combine(): return jnp.stack([east_part, north_part])]
    dot_general x2 -> x0, matrix products: 5.89 us -> none  [the longest x1 3.54 us: on_device(): jnp.einsum('cyx,xj->cyj', channels, banded(n_cols + 2 * R, n_cols), preci...]
    pallas_call x0 -> x3, Pallas kernels: none -> 3.25 us  [the longest x1 2.52 us: on_device(): pl.pallas_call(functools.partial(filter_kernel, geom), out_shape=shape((2...]
    reshape x2 -> x0, local copies, waits for them, and re-layouts: 3.24 us -> none  [unpack(): repeated = jnp.repeat(wet_bits, 30, axis=0)]
    ppermute x4 -> x3, waiting for transfers between devices: 0.01 us -> 2.34 us  [the longest x1 1.74 us: swap(): lax.ppermute(outer, ('tile', 'sub'), pairs)]
    convert_element_type x3 -> x0, other arithmetic: 1.96 us -> none  [the longest x2 1.95 us: unpack(): return (jnp.right_shift(repeated, shifts) & 1).astype(jnp.float32)]
    unnamed x5 -> x8, local copies, waits for them, and re-layouts: 1 us -> 2.89 us
  transfers between devices with their start and end apart: 4 -> 3, of which waited for: 0 -> 2; matrix products, arithmetic and copies ran while one was open for 16% -> 4% of each run, Pallas kernels for 0% -> 0%
where the time goes in v1:
time: 17.2 us; the launch traced here: 16.9 us
  starting transfers between devices  6.33 us (37%)
  local copies, waits for them, and re-layouts  3.53 us (21%)
  Pallas kernels  3.25 us (19%)
  waiting for transfers between devices  2.34 us (14%)
  other arithmetic  0.72 us (4%)
  between operations  0.68 us (4%)
    ppermute x1, starting transfers between devices, on_device(): before = lax.ppermute(rows, 'row', [(0, 1), (1, 0)])  3.03 us
    unnamed x8, local copies, waits for them, and re-layouts  2.89 us
    pallas_call x1, Pallas kernels, on_device(): pl.pallas_call(functools.partial(filter_kernel, geom), out_shape=shape((2...  2.52 us
    ppermute x1, starting transfers between devices, swap(): lax.ppermute(inner, 'sub', beside)  1.83 us
    ppermute x1, waiting for transfers between devices, swap(): lax.ppermute(outer, ('tile', 'sub'), pairs)  1.74 us
    ppermute x1, starting transfers between devices, swap(): lax.ppermute(outer, ('tile', 'sub'), pairs)  1.47 us
    reduce_sum x1, other arithmetic, seam_order(): return jnp.sum(jnp.where(smaller, weight, 0))  0.71 us
    pallas_call x1, local copies, waits for them, and re-layouts, on_device(): pl.pallas_call(functools.partial(filter_kernel, geom), out_shape=shape((2...  0.64 us
  transfers between devices with their start and end apart: 3, of which 2 were waited for; matrix products, arithmetic and copies ran while one was open for 4% of the time, Pallas kernels for 0%

profile of v1, /device:TPU:0, one launch (start us, length us, event | category | flops | bytes accessed | tf_op | source)
XLA Modules:
  0.0 16.9 jit_solution(2936942680485113161)
XLA Ops:
  0.0 0.0 copy-start
  0.0 0.9 %copy-done = f32[2,120,120]{2,1,0:T(8,128)S(1)} copy-done((f32[2,120,120]{2,1,0:T(8,128)S(1)}, f32[2,120,120]{2,1,0:T(8,128)}, u32[]{:S(2)}) %copy-start) | copy-done | bytes 115224
  0.9 0.0 copy-start.1
  0.9 0.7 %copy-done.1 = s32[4]{0:T(128)S(1)} copy-done((s32[4]{0:T(128)S(1)}, s32[4]{0:T(128)}, u32[]{:S(2)}) %copy-start.1) | copy-done | bytes 40
  1.6 0.0 copy-start.2
  1.6 0.7 %copy-done.2 = s32[4,120]{1,0:T(4,128)S(1)} copy-done((s32[4,120]{1,0:T(4,128)S(1)}, s32[4,120]{1,0:T(4,128)}, u32[]{:S(2)}) %copy-start.2) | copy-done | bytes 1944
  2.2 0.0 copy-start.3
  2.2 0.7 %copy-done.3 = s32[4]{0:T(128)S(1)} copy-done((s32[4]{0:T(128)S(1)}, s32[4]{0:T(128)}, u32[]{:S(2)}) %copy-start.3) | copy-done | bytes 40
  2.9 0.6 %mask.1 = (f32[2,120,128]{2,1,0:T(8,128)S(1)}, f32[2,40,128]{2,1,0:T(8,128)S(1)}, f32[120,128]{1,0:T(8,128)S(1)}, f32[8,128]{1,0:T(8,128)S(1)}) custom-call(f32[2,120,120]{2,1,0:T(8,128)S(1)} %copy-done, s32[4,120]{1,0:T(4,128)S(1)} %copy-done.2, s32[4]{0:T(128)S(1)} %copy-done.1, s32[4]{0:T(128)S(1)} %copy-done.3), custom_call_target="tpu_custom_call" | custom-call | tf_op jit(solution)/shard_map/mask/pallas_call | solution.py:293
  3.5 3.0 %collective-permute-start.48 = (f32[2,40,128]{2,1,0:T(8,128)S(1)}, f32[2,40,128]{2,1,0:T(8,128)S(1)}, u32[]{:S(2)}, u32[]{:S(2)}) collective-permute-start(f32[2,40,128]{2,1,0:T(8,128)S(1)} %get-tuple-element.159), channel_id=1, source_target_pairs={{0,2},{2,0},{1,3},{3,1},{4,6},{6,4},{5,7},{7,5},{8,10},{10,8},{9,1... | collective-permute-start | bytes 122888 | tf_op jit(solution)/shard_map/ppermute | solution.py:307
  6.5 0.7 %select_reduce_fusion = s32[]{:T(128)} fusion(s32[4]{0:T(128)S(1)} %compare_select_fusion, s32[4]{0:T(128)S(1)} %copy-done.1, pred[4]{0:T(512)(128)(4,1)S(1)} %get-tuple-element.167, pred[4]{0:T(512)(128)(4,1)S(1)} %get-tuple-element.168, pred[4]{0:T(512)(128)(4,1)S(1)} %iota_compare_fusion.3), kind=kLoop, calls=%fused_computation | loop fusion | flops 127 | bytes 48 | tf_op jit(solution)/shard_map/reduce_sum | solution.py:252
  7.9 0.6 %collective-permute-done.48.before.after = f32[2,40,128]{2,1,0:T(8,128)S(1)} collective-permute-done((f32[2,40,128]{2,1,0:T(8,128)S(1)}, f32[2,40,128]{2,1,0:T(8,128)S(1)}, u32[]{:S(2)}, u32[]{:S(2)}) %collective-permute-start.48) | collective-permute-done | bytes 40992 | tf_op jit(solution)/shard_map/ppermute | solution.py:307
  8.5 0.1 extend.1
  8.7 5.1 %conditional.1 = (f32[160,128]{1,0:T(8,128)}, f32[160,128]{1,0:T(8,128)}) conditional(s32[]{:T(128)} %clamp.3, (f32[160,128]{1,0:T(8,128)S(1)}, f32[160,128]{1,0:T(8,128)S(1)}) %tuple.101, (f32[160,128]{1,0:T(8,128)S(1)}, f32[160,128]{1,0:T(8,128)S(1)}) %tuple.101, (f32[160,128]{1,0:T(8,128)S(1)}, ...), branch_computations={%region_1.2_spmd, %region_2.3_spmd, %region_3.4_spmd, %region_4.5_... | conditional | bytes 655456 | solution.py:272
  8.7 1.5 %collective-permute-start.28 = (f32[160,128]{1,0:T(8,128)S(1)}, f32[160,128]{1,0:T(8,128)}, u32[]{:S(2)}, u32[]{:S(2)}) collective-permute-start(f32[160,128]{1,0:T(8,128)S(1)} %get-tuple-element.129), channel_id=1, source_target_pairs={{1,8},{8,1},{5,4},{4,5},{9,0},{0,9},{13,12},{12,13},{3,10},{10,3},... | collective-permute-start | bytes 245768 | tf_op jit(solution)/shard_map/cond/branch_14_fun/ppermute | solution.py:265
  10.2 1.8 %collective-permute-start.29 = (f32[160,128]{1,0:T(8,128)S(1)}, f32[160,128]{1,0:T(8,128)}, u32[]{:S(2)}, u32[]{:S(2)}) collective-permute-start(f32[160,128]{1,0:T(8,128)S(1)} %get-tuple-element.130), channel_id=1, source_target_pairs={{0,1},{1,0},{2,3},{3,2},{4,5},{5,4},{6,7},{7,6},{8,9},{9,8},{10,11... | collective-permute-start | bytes 245768 | tf_op jit(solution)/shard_map/cond/branch_14_fun/ppermute | solution.py:266
  12.0 1.7 %collective-permute-done.28 = f32[160,128]{1,0:T(8,128)} collective-permute-done((f32[160,128]{1,0:T(8,128)S(1)}, f32[160,128]{1,0:T(8,128)}, u32[]{:S(2)}, u32[]{:S(2)}) %collective-permute-start.28) | collective-permute-done | bytes 81952 | tf_op jit(solution)/shard_map/cond/branch_14_fun/ppermute | solution.py:265
  13.7 0.0 collective-permute-done.29
  13.7 2.5 %filter.1 = f32[2,30,30]{2,1,0:T(8,128)S(1)} custom-call(f32[2,160,128]{2,1,0:T(8,128)S(1)} %get-tuple-element.160.extended, f32[160,128]{1,0:T(8,128)} %get-tuple-element.163.seam, f32[160,128]{1,0:T(8,128)} %get-tuple-element.164.beside, f32[120,128]{1,0:T(8,128)S(1)} %get-tuple-element.165.wet, f32[8,128]{1,0:T(8,128)S(1)} %get-tuple-element.166.turn), custom_call_target="tpu_custom_call" | custom-call | tf_op jit(solution)/shard_map/filter/pallas_call | solution.py:329
  16.2 0.6 %copy.6 = f32[2,30,30]{2,0,1:T(2,128)} copy(f32[2,30,30]{2,1,0:T(8,128)S(1)} %filter.1) | data formatting | bytes 14400 | tf_op jit(solution)/shard_map/filter/pallas_call | solution.py:329
  (3 shorter events, 0.0 us)
Async XLA Ops:
  0.0 0.9 %copy-start = (f32[2,120,120]{2,1,0:T(8,128)S(1)}, f32[2,120,120]{2,1,0:T(8,128)}, u32[]{:S(2)}) copy-start(f32[2,120,120]{2,1,0:T(8,128)} %velocity.1) | copy-start | bytes 345604
  0.9 0.7 %copy-start.1 = (s32[4]{0:T(128)S(1)}, s32[4]{0:T(128)}, u32[]{:S(2)}) copy-start(s32[4]{0:T(128)} %east_face.1) | copy-start | bytes 52
  1.6 0.7 %copy-start.2 = (s32[4,120]{1,0:T(4,128)S(1)}, s32[4,120]{1,0:T(4,128)}, u32[]{:S(2)}) copy-start(s32[4,120]{1,0:T(4,128)} %wet_bits.1) | copy-start | bytes 5764
  2.2 0.7 %copy-start.3 = (s32[4]{0:T(128)S(1)}, s32[4]{0:T(128)}, u32[]{:S(2)}) copy-start(s32[4]{0:T(128)} %seam_turn.1) | copy-start | bytes 52
  3.5 5.0 %collective-permute-start.48 = (f32[2,40,128]{2,1,0:T(8,128)S(1)}, f32[2,40,128]{2,1,0:T(8,128)S(1)}, u32[]{:S(2)}, u32[]{:S(2)}) collective-permute-start(f32[2,40,128]{2,1,0:T(8,128)S(1)} %get-tuple-element.159), channel_id=1, source_target_pairs={{0,2},{2,0},{1,3},{3,1},{4,6},{6,4},{5,7},{7,5},{8,10},{10,8},{9,1... | collective-permute-start | bytes 122888 | tf_op jit(solution)/shard_map/ppermute | solution.py:307
  8.7 5.0 %collective-permute-start.28 = (f32[160,128]{1,0:T(8,128)S(1)}, f32[160,128]{1,0:T(8,128)}, u32[]{:S(2)}, u32[]{:S(2)}) collective-permute-start(f32[160,128]{1,0:T(8,128)S(1)} %get-tuple-element.129), channel_id=1, source_target_pairs={{1,8},{8,1},{5,4},{4,5},{9,0},{0,9},{13,12},{12,13},{3,10},{10,3},... | collective-permute-start | bytes 245768 | tf_op jit(solution)/shard_map/cond/branch_14_fun/ppermute | solution.py:265
  10.2 3.6 %collective-permute-start.29 = (f32[160,128]{1,0:T(8,128)S(1)}, f32[160,128]{1,0:T(8,128)}, u32[]{:S(2)}, u32[]{:S(2)}) collective-permute-start(f32[160,128]{1,0:T(8,128)S(1)} %get-tuple-element.130), channel_id=1, source_target_pairs={{0,1},{1,0},{2,3},{3,2},{4,5},{5,4},{6,7},{7,6},{8,9},{9,8},{10,11... | collective-permute-start | bytes 245768 | tf_op jit(solution)/shard_map/cond/branch_14_fun/ppermute | solution.py:266
